TPU v7x, 32 devices: a whole 2x2x4 slice. The times are simulated.
32 devices in a mesh: ctx: 8 (over z, x), tp: 4 (over y, core).
Axes of the slice: x: 2, y: 2, z: 4, core: 2. Of those that a mesh axis runs over, the one named last changes fastest.
Arguments:
- inputs: bfloat16 [4096, 768], P(('ctx', 'tp')), may hold values from -6 to 6
- positions: int32 [4096], P('ctx'), may hold values from 0 to 3071, as said below
- attn_scale: float32 [768], replicated, may hold values from 0.1 to 1.9
- attn_shift: float32 [768], replicated, may hold values from -4 to 4
- mlp_scale: float32 [768], replicated, may hold values from 0.1 to 1.9
- mlp_shift: float32 [768], replicated, may hold values from -4 to 4
- qkv_weight: bfloat16 [768, 3, 768], P(None, None, 'tp'), may hold values from -0.21875 to 0.21875
- qv_bias: float32 [2, 768], P(None, 'tp'), may hold values from -4 to 4
- dense_weight: bfloat16 [768, 768], P('tp'), may hold values from -1.75 to 1.75
- dense_bias: float32 [768], replicated, may hold values from -5 to 5
- up_weight: bfloat16 [768, 3072], P(None, 'tp'), may hold values from -0.21875 to 0.21875
- up_bias: float32 [3072], P('tp'), may hold values from -4 to 4
- down_weight: bfloat16 [3072, 768], P('tp'), may hold values from -0.109375 to 0.109375
- down_bias: float32 [768], replicated, may hold values from -5 to 5
- cotangent: bfloat16 [4096, 768], P(('ctx', 'tp')), may hold values from -6 to 6
Outputs:
- output: bfloat16 [4096, 768], P(('ctx', 'tp'))
- grad_input: float32 [4096, 768], P(('ctx', 'tp'))
- grad_attn_scale: float32 [768], replicated
- grad_attn_shift: float32 [768], replicated
- grad_mlp_scale: float32 [768], replicated
- grad_mlp_shift: float32 [768], replicated
- grad_qkv: float32 [768, 3, 768], P(None, None, 'tp')
- grad_qv_bias: float32 [2, 768], P(None, 'tp')
- grad_dense: float32 [768, 768], P('tp')
- grad_dense_bias: float32 [768], replicated
- grad_up: float32 [768, 3072], P(None, 'tp')
- grad_up_bias: float32 [3072], P('tp')
- grad_down: float32 [3072, 768], P('tp')
- grad_down_bias: float32 [768], replicated
Inputs may be any that keep to these rules, and one draw needn't show every extreme that they name: The sequence holds three documents; positions count from 0 at each document's first token and rise by one along it; the second document has 3072 tokens and starts at a token between 1 and 1023.
All inputs are finite; a program needn't handle non-finite values.
Results may differ from a plain program's by a relative error of at most 0.025.
Values may be sent and summed in bfloat16 or wider, within the bound.
A program may use at most 128 MiB of HBM per device.

v0:
```python
import math
import jax
import jax.numpy as jnp
from jax import lax
from jax.sharding import PartitionSpec as P

D = 768
HD = 64
ROT = 16
norm_eps = 1e-05


def layer_norm(values, scale, shift):
    mean_value = jnp.mean(values, axis=-1, keepdims=True)
    centred = values - mean_value
    variance = jnp.mean(centred * centred, axis=-1, keepdims=True)
    inv_std = lax.rsqrt(variance + norm_eps)
    normal_part = centred * inv_std
    return (normal_part * scale + shift, normal_part, inv_std)


def norm_backward(grad_normed, normal_part, inv_std, scale):
    grad_hat = grad_normed * scale
    mean_grad = jnp.mean(grad_hat, axis=-1, keepdims=True)
    mean_mixed = jnp.mean(grad_hat * normal_part, axis=-1, keepdims=True)
    return inv_std * (grad_hat - mean_grad - normal_part * mean_mixed)


def rotary_tables(positions):
    freqs = 10000.0 ** (-jnp.arange(0, ROT, 2).astype(jnp.float32) / ROT)
    angles = positions.astype(jnp.float32)[:, None] * freqs[None, :]
    angles = jnp.concatenate([angles, angles], axis=1)
    return (jnp.cos(angles), jnp.sin(angles))


def rotate(tensor, cosines, sines):
    part = tensor[..., :ROT]
    half = ROT // 2
    turned = jnp.concatenate([-part[..., half:], part[..., :half]], axis=-1)
    spun = part * cosines[:, None, :] + turned * sines[:, None, :]
    return jnp.concatenate([spun, tensor[..., ROT:]], axis=-1)


def gelu_grad(pre_act):
    cumulative = 0.5 * (1.0 + jax.scipy.special.erf(pre_act * 0.7071067811865476))
    density = jnp.exp(-0.5 * pre_act * pre_act) * 0.3989422804014327
    return cumulative + pre_act * density


def block_length(length):
    return math.gcd(length, 1024)


def local(
    inputs,
    positions,
    attn_scale,
    attn_shift,
    mlp_scale,
    mlp_shift,
    qkv_weight,
    qv_bias,
    dense_weight,
    dense_bias,
    up_weight,
    up_bias,
    down_weight,
    down_bias,
    cotangent,
):
    local_width = qkv_weight.shape[2]
    head_count = local_width // HD
    score_scale = HD ** (-0.5)
    resid = inputs.astype(jnp.float32)
    normed_one, hat_one, std_one = layer_norm(resid, attn_scale, attn_shift)
    normed_two, hat_two, std_two = layer_norm(resid, mlp_scale, mlp_shift)
    attn_in, mlp_in = (
        lax.all_gather(normed_one.astype(jnp.bfloat16), "tp", axis=0, tiled=True),
        lax.all_gather(normed_two.astype(jnp.bfloat16), "tp", axis=0, tiled=True),
    )
    block_rows = attn_in.shape[0]
    proj = jnp.dot(
        attn_in, qkv_weight.reshape(D, 3 * local_width), preferred_element_type=jnp.float32
    )
    proj = proj.reshape(block_rows, 3, head_count, HD)
    cosines, sines = rotary_tables(positions)
    queries = rotate(proj[:, 0] + qv_bias[0].reshape(head_count, HD), cosines, sines).astype(
        jnp.bfloat16
    )
    keys_rot = rotate(proj[:, 1], cosines, sines).astype(jnp.bfloat16)
    values = (proj[:, 2] + qv_bias[1].reshape(head_count, HD)).astype(jnp.bfloat16)
    own_start = lax.axis_index("ctx") * block_rows
    query_pos = own_start + jnp.arange(block_rows, dtype=jnp.int32)
    first_key = query_pos - positions
    last_query = query_pos[block_rows - 1]
    earliest_key = jnp.min(first_key)

    def visible_mask(start_row, length):
        key_pos = start_row + jnp.arange(length, dtype=jnp.int32)
        return (key_pos[None, :] <= query_pos[:, None]) & (key_pos[None, :] >= first_key[:, None])

    def reachable(start_row, length):
        return (start_row <= last_query) & (start_row + length - 1 >= earliest_key)

    def attend_block(running, key_block, value_block, start_row):
        row_max, row_sum, accumulated = running
        visible = visible_mask(start_row, key_block.shape[0])
        scores = (
            jnp.einsum("qhd,khd->hqk", queries, key_block, preferred_element_type=jnp.float32)
            * score_scale
        )
        scores = jnp.where(visible[None], scores, -1e30)
        new_max = jnp.maximum(row_max, jnp.max(scores, axis=-1))
        weights = jnp.where(visible[None], jnp.exp(scores - new_max[..., None]), 0.0)
        factor = jnp.exp(row_max - new_max)
        row_sum = row_sum * factor + jnp.sum(weights, axis=-1)
        accumulated = accumulated * factor[..., None] + jnp.einsum(
            "hqk,khd->hqd",
            weights.astype(jnp.bfloat16),
            value_block,
            preferred_element_type=jnp.float32,
        )
        return (new_max, row_sum, accumulated)

    initial = (
        jnp.full((head_count, block_rows), -1e30, jnp.float32),
        jnp.zeros((head_count, block_rows), jnp.float32),
        jnp.zeros((head_count, block_rows, HD), jnp.float32),
    )
    running = initial
    key_rows = lax.all_gather(keys_rot, "ctx", axis=0, tiled=True)
    value_rows = lax.all_gather(values, "ctx", axis=0, tiled=True)
    length = key_rows.shape[0]
    attend_step_rows = block_length(length)
    steps_count = length // attend_step_rows
    key_blocks = key_rows.reshape(steps_count, attend_step_rows, head_count, HD)
    value_blocks = value_rows.reshape(steps_count, attend_step_rows, head_count, HD)

    def one_step(current, inputs_step):
        key_block, value_block, number = inputs_step
        block_start = number * attend_step_rows

        def attend_now(state):
            return attend_block(state, key_block, value_block, block_start)

        def keep_state(state):
            return state

        return (
            lax.cond(reachable(block_start, attend_step_rows), attend_now, keep_state, current),
            None,
        )

    running, unused = lax.scan(
        one_step, running, (key_blocks, value_blocks, jnp.arange(steps_count, dtype=jnp.int32))
    )
    row_max, row_sum, accumulated = running
    attended = jnp.transpose(accumulated / row_sum[..., None], (1, 0, 2)).astype(jnp.bfloat16)
    log_total = row_max + jnp.log(row_sum)
    attended_flat = attended.reshape(block_rows, local_width)
    attn_part = jnp.dot(attended_flat, dense_weight, preferred_element_type=jnp.float32)
    pre_act = jnp.dot(mlp_in, up_weight, preferred_element_type=jnp.float32) + up_bias
    activation = jax.nn.gelu(pre_act, approximate=False).astype(jnp.bfloat16)
    mlp_part = jnp.dot(activation, down_weight, preferred_element_type=jnp.float32)
    branch_sum = lax.psum_scatter(attn_part + mlp_part, "tp", scatter_dimension=0, tiled=True)
    output = (resid + branch_sum + dense_bias + down_bias).astype(jnp.bfloat16)
    grad_out = cotangent.astype(jnp.float32)
    bias_grad = jnp.sum(grad_out, axis=0)
    grad_full = lax.all_gather(cotangent, "tp", axis=0, tiled=True)
    grad_down = jnp.dot(activation.T, grad_full, preferred_element_type=jnp.float32)
    grad_act = jnp.dot(grad_full, down_weight.T, preferred_element_type=jnp.float32)
    grad_pre = grad_act * gelu_grad(pre_act)
    grad_up_bias = jnp.sum(grad_pre, axis=0)
    grad_pre_low = grad_pre.astype(jnp.bfloat16)
    grad_up = jnp.dot(mlp_in.T, grad_pre_low, preferred_element_type=jnp.float32)
    grad_mlp_in = jnp.dot(grad_pre_low, up_weight.T, preferred_element_type=jnp.float32)
    grad_dense = jnp.dot(attended_flat.T, grad_full, preferred_element_type=jnp.float32)
    grad_attended = jnp.dot(grad_full, dense_weight.T, preferred_element_type=jnp.float32)
    grad_attended = grad_attended.astype(jnp.bfloat16).reshape(block_rows, head_count, HD)
    delta_rows = jnp.transpose(
        jnp.sum(grad_attended.astype(jnp.float32) * attended.astype(jnp.float32), axis=-1)
    )

    def score_grads(query_rows, grad_rows, log_rows, delta_part, key_block, value_block, visible):
        scores = (
            jnp.einsum("qhd,khd->hqk", query_rows, key_block, preferred_element_type=jnp.float32)
            * score_scale
        )
        weights = jnp.where(visible[None], jnp.exp(scores - log_rows[..., None]), 0.0)
        grad_weights = jnp.einsum(
            "qhd,khd->hqk", grad_rows, value_block, preferred_element_type=jnp.float32
        )
        grad_scores = (weights * (grad_weights - delta_part[..., None])).astype(jnp.bfloat16)
        return (weights.astype(jnp.bfloat16), grad_scores)

    key_back, value_back = (
        lax.all_gather(keys_rot, "ctx", axis=0, tiled=True),
        lax.all_gather(values, "ctx", axis=0, tiled=True),
    )
    total_rows = key_back.shape[0]
    step_rows = block_length(total_rows)
    steps_count = total_rows // step_rows
    back_inputs = (
        key_back.reshape(steps_count, step_rows, head_count, HD),
        value_back.reshape(steps_count, step_rows, head_count, HD),
        jnp.arange(steps_count, dtype=jnp.int32),
    )
    zero_query = jnp.zeros((block_rows, head_count, HD), jnp.float32)

    def back_step(query_grad, inputs_step):
        key_block, value_block, number = inputs_step
        block_start = number * step_rows

        def with_terms(grad_now):
            visible = visible_mask(block_start, step_rows)
            weights_low, grad_scores = score_grads(
                queries, grad_attended, log_total, delta_rows, key_block, value_block, visible
            )
            grad_now = (
                grad_now
                + jnp.einsum(
                    "hqk,khd->qhd", grad_scores, key_block, preferred_element_type=jnp.float32
                )
                * score_scale
            )
            key_part = (
                jnp.einsum("hqk,qhd->khd", grad_scores, queries, preferred_element_type=jnp.float32)
                * score_scale
            )
            value_part = jnp.einsum(
                "hqk,qhd->khd", weights_low, grad_attended, preferred_element_type=jnp.float32
            )
            joined = jnp.concatenate(
                [
                    key_part.reshape(step_rows, local_width),
                    value_part.reshape(step_rows, local_width),
                ],
                axis=1,
            )
            return (grad_now, joined)

        def without_terms(grad_now):
            return (grad_now, jnp.zeros((step_rows, 2 * local_width), jnp.float32))

        return lax.cond(reachable(block_start, step_rows), with_terms, without_terms, query_grad)

    query_grad, key_terms = lax.scan(back_step, zero_query, back_inputs)
    key_terms = key_terms.reshape(total_rows, 2 * local_width)
    own_terms = lax.psum_scatter(key_terms, "ctx", scatter_dimension=0, tiled=True)
    key_grad = own_terms[:, :local_width].reshape(block_rows, head_count, HD)
    value_grad = own_terms[:, local_width:].reshape(block_rows, head_count, HD)
    grad_query_pre = rotate(query_grad, cosines, -sines)
    grad_key_pre = rotate(key_grad, cosines, -sines)
    qv_bias_grad = jnp.stack(
        [
            jnp.sum(grad_query_pre, axis=0).reshape(local_width),
            jnp.sum(value_grad, axis=0).reshape(local_width),
        ]
    )
    grad_proj = jnp.stack([grad_query_pre, grad_key_pre, value_grad], axis=1)
    grad_proj = grad_proj.reshape(block_rows, 3 * local_width).astype(jnp.bfloat16)
    grad_qkv = jnp.dot(attn_in.T, grad_proj, preferred_element_type=jnp.float32).reshape(
        D, 3, local_width
    )
    grad_attn_in = jnp.dot(
        grad_proj, qkv_weight.reshape(D, 3 * local_width).T, preferred_element_type=jnp.float32
    )
    own_attn, own_mlp = (
        lax.psum_scatter(grad_attn_in, "tp", scatter_dimension=0, tiled=True),
        lax.psum_scatter(grad_mlp_in, "tp", scatter_dimension=0, tiled=True),
    )
    grad_input = grad_out + norm_backward(own_attn, hat_one, std_one, attn_scale)
    grad_input = grad_input + norm_backward(own_mlp, hat_two, std_two, mlp_scale)
    norm_sums = lax.psum(
        (
            jnp.sum(own_attn * hat_one, axis=0),
            jnp.sum(own_attn, axis=0),
            jnp.sum(own_mlp * hat_two, axis=0),
            jnp.sum(own_mlp, axis=0),
            bias_grad,
        ),
        ("ctx", "tp"),
    )
    weight_sums = lax.psum(
        (grad_qkv, qv_bias_grad, grad_dense, grad_up, grad_up_bias, grad_down), "ctx"
    )
    return (
        output,
        grad_input,
        norm_sums[0],
        norm_sums[1],
        norm_sums[2],
        norm_sums[3],
        weight_sums[0],
        weight_sums[1],
        weight_sums[2],
        norm_sums[4],
        weight_sums[3],
        weight_sums[4],
        weight_sums[5],
        norm_sums[4],
    )


def solution(mesh):
    in_specs = (
        P(("ctx", "tp"), None),
        P("ctx"),
        P(),
        P(),
        P(),
        P(),
        P(None, None, "tp"),
        P(None, "tp"),
        P("tp", None),
        P(),
        P(None, "tp"),
        P("tp"),
        P("tp", None),
        P(),
        P(("ctx", "tp"), None),
    )
    out_specs = (
        P(("ctx", "tp"), None),
        P(("ctx", "tp"), None),
        P(),
        P(),
        P(),
        P(),
        P(None, None, "tp"),
        P(None, "tp"),
        P("tp", None),
        P(),
        P(None, "tp"),
        P("tp"),
        P("tp", None),
        P(),
    )
    return jax.shard_map(local, mesh=mesh, in_specs=in_specs, out_specs=out_specs, check_vma=False)
```

profile of v0, /device:TPU:0, one launch (start us, length us, event | category | flops | bytes accessed | tf_op | source)
XLA Modules:
  0.0 690.6 jit_solution(9488253124478135631)
XLA Ops:
  9.6 1.9 fusion.74
  11.5 10.1 %all_gather.17 = bf16[512,768]{1,0:T(8,128)(2,1)S(1)} all-gather(bf16[128,768]{1,0:T(8,128)(2,1)S(1)} %get-tuple-element.958), channel_id=1, replica_groups=mesh['ctx'=8,'tp'=4] {'tp'}, dimensions={0}, use_global_device_ids=true | all-gather | bytes 983040 | tf_op jit(solution)/shard_map/all_gather | solution.py:78
  27.7 8.7 %all_gather.21 = bf16[512,768]{1,0:T(8,128)(2,1)S(1)} all-gather(bf16[128,768]{1,0:T(8,128)(2,1)S(1)} %copy-done.29), channel_id=1, replica_groups=mesh['ctx'=8,'tp'=4] {'tp'}, dimensions={0}, use_global_device_ids=true | all-gather | bytes 983040 | tf_op jit(solution)/shard_map/all_gather | solution.py:169
  37.7 33.9 %all-gather.3.cloned.1.call-done = bf16[4096,3,64]{0,2,1:T(8,128)(2,1)} async-done(((bf16[512,3,64]{0,2,1:T(8,128)(2,1)}), bf16[4096,3,64]{0,2,1:T(8,128)(2,1)}) %all-gather.3.cloned.1.call-update) | async-done | bytes 1572880 | tf_op jit(solution)/shard_map/all_gather | solution.py:131
  71.6 1.6 copy.75
  73.2 43.7 %all-gather.5.cloned.1.call-done = bf16[4096,3,64]{0,2,1:T(8,128)(2,1)} async-done(((bf16[512,3,64]{0,2,1:T(8,128)(2,1)}), bf16[4096,3,64]{0,2,1:T(8,128)(2,1)}) %all-gather.5.cloned.1.call-update) | async-done | bytes 1572880 | tf_op jit(solution)/shard_map/all_gather | solution.py:132
  116.9 2.7 copy.74
  120.1 23.0 %while.39 = (s32[]{:T(128)}, f32[3,512]{1,0:T(4,128)S(1)}, f32[3,512]{1,0:T(4,128)S(1)}, f32[3,512,64]{1,2,0:T(8,128)S(1)}, s32[4]{0:T(128)}, /*index=5*/s32[]{:...) while((s32[]{:T(128)}, f32[3,512]{1,0:T(4,128)S(1)}, ...), condition=%wide.region_8.9_spmd.clone, body=%wide.region_3.8_spmd.clone.sunk | while | flops 424874496 | bytes 22858608 | solution.py:154
  120.1 1.2 dynamic_slice.82
  123.9 7.8 %conditional.6 = ((f32[3,512]{1,0:T(4,128)S(1)}, f32[3,512]{1,0:T(4,128)S(1)}, f32[3,512,64]{1,2,0:T(8,128)S(1)})) conditional(s32[]{:T(128)} %convert_element_type.207, (f32[3,512]{1,0:T(4,128)S(1)}, f32[3,512]{1,0:T(4,128)S(1)}, f32[3,512,64]{1,2,0:T(8,128)S(1)}) %tuple.156, (s32[]{:T(128)}, s32[]{:T(128)}, s32[512]{0:T(512)}, ...), branch_computations={%region_4.4_spmd, %region_5.7_spmd} | conditional | flops 424874496 | bytes 22856236 | solution.py:150
  125.8 1.4 fusion.4
  127.2 1.6 fusion.6
  128.8 3.0 fusion.10
  143.7 1.4 multiply_reduce_fusion
  145.1 37.2 %while.40 = (s32[]{:T(128)}, f32[512,3,64]{0,2,1:T(8,128)S(1)}, f32[4,1024,384]{2,1,0:T(8,128)}, s32[4]{0:T(128)S(1)}, s32[]{:T(128)}, /*index=5*/s32[]{:T(128)}...) while((s32[]{:T(128)}, f32[512,3,64]{0,2,1:T(8,128)S(1)}, ...), condition=%wide.region_14.15_spmd.clone, body=%wide.region_11.14_spmd.clone.sunk | while | flops 1024722432 | bytes 56325616 | solution.py:247
  147.8 8.3 %conditional.7 = (f32[512,3,64]{0,2,1:T(8,128)S(1)}, f32[1,1024,384]{1,2,0:T(8,128)S(1)}) conditional(s32[]{:T(128)} %convert_element_type.208, f32[512,3,64]{0,2,1:T(8,128)S(1)} %get-tuple-element.1217, (s32[]{:T(128)}, s32[]{:T(128)}, s32[512]{0:T(512)}, bf16[4,1024,3,64]{1,3,2,0:T(8,128)(2,1)S(1)}, s32[]{:T(128)}, ...), branch_computations={%region_12.12_spmd, %region_13.13_spmd} | conditional | flops 1024722432 | bytes 37448308 | solution.py:245
  149.4 3.3 fusion.23
  153.4 1.5 fusion.25
  156.1 1.6 copy.77
  157.7 2.8 constant_dynamic-update-slice_fusion.2
  163.4 1.6 copy.77
  165.0 2.8 constant_dynamic-update-slice_fusion.2
  170.6 1.6 copy.77
  172.3 2.8 constant_dynamic-update-slice_fusion.2
  177.9 1.6 copy.77
  179.5 2.8 constant_dynamic-update-slice_fusion.2
  183.3 8.7 %all_gather.20 = bf16[512,768]{1,0:T(8,128)(2,1)S(1)} all-gather(bf16[128,768]{1,0:T(8,128)(2,1)S(1)} %copy-done.31), channel_id=1, replica_groups=mesh['ctx'=8,'tp'=4] {'tp'}, dimensions={0}, use_global_device_ids=true | all-gather | bytes 983040 | tf_op jit(solution)/shard_map/all_gather | solution.py:79
  192.0 4.2 fusion.44
  198.3 2.0 fusion.93
  201.8 144.9 %reduce-scatter.7.cloned.1.call-done = f32[512,384]{1,0:T(8,128)} async-done(((f32[4096,384]{1,0:T(8,128)}), f32[512,384]{1,0:T(8,128)}) %reduce-scatter.7.cloned.1.call-update) | async-done | bytes 786448 | tf_op jit(solution)/shard_map/reduce_scatter | solution.py:249
  346.7 2.0 slice.122
  348.6 1.8 copy.47
  351.4 1.3 copy.46
  354.5 2.0 fusion.111
  357.9 2.0 convolution_add_fusion
  361.0 3.3 fusion.91
  364.4 2.2 fusion.113
  368.1 1.8 fusion.59
  371.1 20.6 %all-reduce.1 = (f32[2,192]{1,0:T(2,128)}, f32[768]{0:T(1024)}) all-reduce(f32[2,192]{1,0:T(2,128)S(1)} %pad_maximum_fusion.4, f32[768]{0:T(1024)S(1)} %get-tuple-element.970), channel_id=1, replica_groups=mesh['ctx'=8,'tp'=4] {'ctx'}, use_global_device_ids=true, to_apply=%region_33.34 | all-reduce | flops 1152 | bytes 9216 | tf_op jit(solution)/shard_map/psum | solution.py:284
  391.7 15.1 %reduce-scatter.9.cloned.1.call-done = f32[128,768]{1,0:T(8,128)} async-done(((f32[512,768]{1,0:T(8,128)}), f32[128,768]{1,0:T(8,128)}) %reduce-scatter.9.cloned.1.call-update) | async-done | bytes 393232 | tf_op jit(solution)/shard_map/reduce_scatter | solution.py:269
  406.8 1.5 fusion.82
  408.3 28.8 %reduce-scatter.5.cloned.1.call-done = f32[128,768]{1,0:T(8,128)} async-done(((f32[512,768]{1,0:T(8,128)}), f32[128,768]{1,0:T(8,128)}) %reduce-scatter.5.cloned.1.call-update) | async-done | bytes 393232 | tf_op jit(solution)/shard_map/reduce_scatter | solution.py:165
  437.2 2.3 convert_reduce_fusion.1
  439.5 43.0 %all-reduce = (f32[768]{0:T(1024)}, f32[768]{0:T(1024)}, f32[768]{0:T(1024)}, f32[768]{0:T(1024)}, f32[768]{0:T(1024)S(1)}) all-reduce(f32[768]{0:T(1024)S(1)} %get-tuple-element.862, f32[768]{0:T(1024)S(1)} %get-tuple-element.867, f32[768]{0:T(1024)S(1)} %get-tuple-element.871, ...), channel_id=1, replica_groups=mesh['ctx'=8,'tp'=4] {'ctx','tp'}, use_global_device_ids=true, to_apply=%region_23.24 | all-reduce | flops 3840 | bytes 30720 | tf_op jit(solution)/shard_map/psum | solution.py:274
  482.5 193.0 %all-reduce.5.cloned.1.call-done = (f32[768,3,192]{0,2,1:T(8,128)}, f32[192,768]{1,0:T(8,128)}, f32[768,768]{1,0:T(8,128)}, f32[768,768]{1,0:T(8,128)}) async-done(((f32[768,3,192]{0,2,1:T(8,128)}, f32[192,768]{1,0:T(8,128)}, f32[768,768]{1,0:T(8,128)}, f32[768,768]{1,0:T(8,128)}), (f32[768,3,192]{0,2,1:T(8,128)}, f32[192,768]{1,0:T(8,128)}, f32[768,768]{1,0:T(8,128)}, ...) | async-done | bytes 7077904 | tf_op jit(solution)/shard_map/psum | solution.py:284
  676.0 2.9 copy.118
  679.8 1.4 copy.120
  682.3 1.4 copy.121
  (221 shorter events, 40.8 us)
Async XLA Ops:
  7.2 184.8 %copy-start = (bf16[768,768]{1,0:T(8,128)(2,1)S(1)}, bf16[768,768]{1,0:T(8,128)(2,1)}, u32[]{:S(2)}) copy-start(bf16[768,768]{1,0:T(8,128)(2,1)} %param.33) | copy-start | bytes 3538948
  7.2 14.4 %copy-start.12 = (bf16[768,3,192]{0,2,1:T(8,128)(2,1)S(1)}, bf16[768,3,192]{0,2,1:T(8,128)(2,1)}, u32[]{:S(2)}) copy-start(bf16[768,3,192]{0,2,1:T(8,128)(2,1)} %param.29) | copy-start | bytes 2654212
  7.2 64.4 %all-gather.3.cloned.1.call-start = ((), (), s32[]{:S(2)}) async-start(), calls=%async_computation.4 | async-start | bytes 1769472 | tf_op jit(solution)/shard_map/all_gather | solution.py:131
  8.5 13.1 %copy-start.41 = (f32[128]{0:T(128)}, f32[128]{0:T(128)S(1)}, u32[]{:S(2)}) copy-start(f32[128]{0:T(128)S(1)} %broadcast_multiply_fusion.5) | copy-start | bytes 1540
  9.6 12.0 %copy-start.44 = (f32[128]{0:T(128)}, f32[128]{0:T(128)S(1)}, u32[]{:S(2)}) copy-start(f32[128]{0:T(128)S(1)} %add_rsqrt_fusion) | copy-start | bytes 1540
  23.5 4.2 copy-start.29
  24.8 12.5 %copy-start.23 = (bf16[192,768]{1,0:T(8,128)(2,1)S(1)}, bf16[192,768]{1,0:T(8,128)(2,1)}, u32[]{:S(2)}) copy-start(bf16[192,768]{1,0:T(8,128)(2,1)} %param.31) | copy-start | bytes 884740
  25.5 12.2 %copy-start.34 = (f32[512,16]{0,1:T(8,128)}, f32[512,16]{0,1:T(8,128)S(1)}, u32[]{:S(2)}) copy-start(f32[512,16]{0,1:T(8,128)S(1)} %get-tuple-element.966) | copy-start | bytes 98308
  26.2 90.6 %all-gather.5.cloned.1.call-start = ((), (), s32[]{:S(2)}) async-start(), calls=%async_computation.5 | async-start | bytes 1769472 | tf_op jit(solution)/shard_map/all_gather | solution.py:132
  27.0 319.7 %reduce-scatter.7.cloned.1.call-start = ((), (), s32[]{:S(2)}) async-start(), calls=%async_computation.7 | async-start | bytes 7077888 | tf_op jit(solution)/shard_map/reduce_scatter | solution.py:249
  145.1 2.7 copy-start.1
  147.8 1.6 copy-start.40
  147.8 1.6 copy-start.43
  157.7 2.8 copy-start.2
  160.5 2.6 copy-start.1
  165.0 2.8 copy-start.2
  167.8 2.6 copy-start.1
  172.2 2.8 copy-start.2
  175.0 2.6 copy-start.1
  179.5 2.8 copy-start.2
  182.3 9.7 %copy-start.51 = (f32[768]{0:T(1024)S(1)}, f32[768]{0:T(1024)}, u32[]{:S(2)}) copy-start(f32[768]{0:T(1024)} %param.34) | copy-start | bytes 9220
  182.4 209.3 %reduce-scatter.11.cloned.1.call-start = ((), (), s32[]{:S(2)}) async-start(), calls=%async_computation.9 | async-start | bytes 1966080 | tf_op jit(solution)/shard_map/reduce_scatter | solution.py:270
  192.0 4.3 copy-start.7
  192.0 4.3 copy-start.4
  192.0 4.3 copy-start.21
  200.3 206.5 %reduce-scatter.9.cloned.1.call-start = ((), (), s32[]{:S(2)}) async-start(), calls=%async_computation.8 | async-start | bytes 1966080 | tf_op jit(solution)/shard_map/reduce_scatter | solution.py:269
  346.7 3.7 copy-start.18
  351.3 2.2 copy-start.27
  351.4 2.2 copy-start.28
  352.6 1.9 copy-start.13
  354.5 2.1 copy-start.19
  354.5 2.1 copy-start.24
  356.5 80.7 %reduce-scatter.5.cloned.1.call-start = ((), (), s32[]{:S(2)}) async-start(), calls=%async_computation.6 | async-start | bytes 1966080 | tf_op jit(solution)/shard_map/reduce_scatter | solution.py:165
  359.9 315.5 %all-reduce.5.cloned.1.call-start = ((), (), s32[]{:S(2)}) async-start(), calls=%async_computation.10 | async-start | bytes 14155776 | tf_op jit(solution)/shard_map/psum | solution.py:284
  364.4 2.2 copy-start.20
  366.6 1.5 copy-start.10
  369.9 36.9 %copy-start.11 = (bf16[128,768]{1,0:T(8,128)(2,1)S(1)}, bf16[128,768]{1,0:T(8,128)(2,1)}, u32[]{:S(2)}) copy-start(bf16[128,768]{1,0:T(8,128)(2,1)} %param.23) | copy-start | bytes 589828
  369.9 36.9 %copy-start.38 = (f32[768]{0:T(1024)S(1)}, f32[768]{0:T(1024)}, u32[]{:S(2)}) copy-start(f32[768]{0:T(1024)} %param.27) | copy-start | bytes 9220
  369.9 36.9 %copy-start.39 = (f32[768]{0:T(1024)S(1)}, f32[768]{0:T(1024)}, u32[]{:S(2)}) copy-start(f32[768]{0:T(1024)} %param.25) | copy-start | bytes 9220
  369.9 36.9 %copy-start.42 = (f32[128]{0:T(128)S(1)}, f32[128]{0:T(128)}, u32[]{:S(2)}) copy-start(f32[128]{0:T(128)} %copy-done.41) | copy-start | bytes 1540
  369.9 36.9 %copy-start.45 = (f32[128]{0:T(128)S(1)}, f32[128]{0:T(128)}, u32[]{:S(2)}) copy-start(f32[128]{0:T(128)} %copy-done.44) | copy-start | bytes 1540
  369.9 67.2 %copy-start.46 = (f32[768]{0:T(1024)S(1)}, f32[768]{0:T(1024)}, u32[]{:S(2)}) copy-start(f32[768]{0:T(1024)} %param.36) | copy-start | bytes 9220
  369.9 67.2 %copy-start.47 = (f32[768]{0:T(1024)S(1)}, f32[768]{0:T(1024)}, u32[]{:S(2)}) copy-start(f32[768]{0:T(1024)} %param.32) | copy-start | bytes 9220
  370.9 66.3 %copy-start.30 = (bf16[128,768]{1,0:T(8,128)(2,1)S(1)}, bf16[128,768]{1,0:T(8,128)(2,1)}, u32[]{:S(2)}) copy-start(bf16[128,768]{1,0:T(8,128)(2,1)} %param.37) | copy-start | bytes 589828
  482.5 196.5 %copy-start.48 = (f32[768]{0:T(1024)}, f32[768]{0:T(1024)S(1)}, u32[]{:S(2)}) copy-start(f32[768]{0:T(1024)S(1)} %get-tuple-element.1287) | copy-start | bytes 9220
  676.0 3.0 copy-start.33
  676.0 3.8 copy-start.17
  679.8 2.5 copy-start.16
  (17 other events, 16.2 us)
Sparse Core Ops, SparseCore 0:
  26.3 45.2 all-gather.2
  74.2 42.5 all-gather.4
  182.5 164.1 reduce-scatter.6
  349.1 27.2 reduce-scatter.10
  378.7 27.9 reduce-scatter.8
  409.2 27.9 reduce-scatter.4
  442.7 232.6 all-reduce.4
where the time goes:
time: 692 us; the launch traced here: 691 us
  waiting for transfers between devices  460 us (66%)
  blocking collectives  91.1 us (13%)
  local copies, waits for them, and re-layouts  54.8 us (8%)
  matrix products  33.3 us (5%)
  other arithmetic  20.3 us (3%)
  loops' own time  16 us (2%)
  between operations  14.7 us (2%)
    psum x1, waiting for transfers between devices, local(): lax.psum((grad_qkv, qv_bias_grad, grad_dense, grad_up, grad_up_bias, grad...  193 us
    reduce_scatter x1, waiting for transfers between devices, local(): lax.psum_scatter(key_terms, 'ctx', scatter_dimension=0, tiled=True)  145 us
    all_gather x1, waiting for transfers between devices, local(): value_rows = lax.all_gather(values, 'ctx', axis=0, tiled=True)  43.7 us
    psum x1, blocking collectives, local(): lax.psum((jnp.sum(own_attn * hat_one, axis=0), jnp.sum(own_attn, axis=0),...  43 us
    all_gather x1, waiting for transfers between devices, local(): key_rows = lax.all_gather(keys_rot, 'ctx', axis=0, tiled=True)  33.9 us
    reduce_scatter x1, waiting for transfers between devices, local(): lax.psum_scatter(attn_part + mlp_part, 'tp', scatter_dimension=0, tiled=T...  28.8 us
    psum x1, blocking collectives, local(): lax.psum((grad_qkv, qv_bias_grad, grad_dense, grad_up, grad_up_bias, grad...  20.6 us
    dynamic_update_slice x8, local copies, waits for them, and re-layouts, local(): query_grad, key_terms = lax.scan(back_step, zero_query, back_inputs)  17.6 us
  transfers between devices with their start and end apart: 7, of which 6 were waited for; matrix products, arithmetic and copies ran while one was open for 5% of the time, Pallas kernels for 0%

commit v1 on v0

--- a/solution.py
+++ b/solution.py
@@ -129,7 +129,23 @@
     )
     running = initial
     key_rows = lax.all_gather(keys_rot, "ctx", axis=0, tiled=True)
-    value_rows = lax.all_gather(values, "ctx", axis=0, tiled=True)
+
+    def turn_regions(xin):
+        device_axis = "ctx"
+        n_lanes = lax.axis_size(device_axis)
+        blocks_here = [xin]
+        for tick in tuple(range(1, n_lanes)):
+            blocks_here.append(
+                lax.ppermute(
+                    blocks_here[tick - 1],
+                    axis_name=device_axis,
+                    perm=[(pp, (pp - 1) % n_lanes) for pp in range(n_lanes)],
+                )
+            )
+        fresh = jnp.concatenate(blocks_here, 0)
+        return jnp.roll(fresh, lax.axis_index(device_axis) * xin.shape[0], 0)
+
+    value_rows = turn_regions(values)
     length = key_rows.shape[0]
     attend_step_rows = block_length(length)
     steps_count = length // attend_step_rows

time: 692 us -> 670 us (0.968)
  waiting for transfers between devices: 460 us -> 397 us
  starting transfers between devices: 0.29 us -> 33.6 us
  local copies, waits for them, and re-layouts: 54.8 us -> 63.6 us
    all_gather x1, waiting for transfers between devices: 43.7 us -> 9.59 us  [local(): lax.all_gather(values, 'ctx', axis=0, tiled=True)]
    all_gather x1, waiting for transfers between devices: 33.9 us -> 0.01 us  [local(): key_rows = lax.all_gather(keys_rot, 'ctx', axis=0, tiled=True)]
    ppermute x0 -> x7, starting transfers between devices: none -> 33.3 us  [turn_regions(): lax.ppermute(blocks_here[tick - 1], axis_name=device_axis, perm=[(pp, (pp...]
    ppermute x0 -> x7, waiting for transfers between devices: none -> 19 us  [turn_regions(): lax.ppermute(blocks_here[tick - 1], axis_name=device_axis, perm=[(pp, (pp...]
    reduce_scatter x1, waiting for transfers between devices: 145 us -> 132 us  [local(): lax.psum_scatter(key_terms, 'ctx', scatter_dimension=0, tiled=True)]
    unnamed x99 -> x119, local copies, waits for them, and re-layouts: 15.8 us -> 25.8 us
  transfers between devices with their start and end apart: 7 -> 14, of which waited for: 6 -> 11; matrix products, arithmetic and copies ran while one was open for 5% -> 9% of each run, Pallas kernels for 0% -> 0%
where the time goes in v1:
time: 670 us; the launch traced here: 669 us
  waiting for transfers between devices  397 us (59%)
  blocking collectives  89.9 us (13%)
  local copies, waits for them, and re-layouts  63.6 us (9%)
  matrix products  33.9 us (5%)
  starting transfers between devices  33.6 us (5%)
  other arithmetic  19.4 us (3%)
  loops' own time  16.2 us (2%)
  between operations  14.7 us (2%)
    psum x1, waiting for transfers between devices, local(): lax.psum((grad_qkv, qv_bias_grad, grad_dense, grad_up, grad_up_bias, grad...  193 us
    reduce_scatter x1, waiting for transfers between devices, local(): lax.psum_scatter(key_terms, 'ctx', scatter_dimension=0, tiled=True)  132 us
    psum x1, blocking collectives, local(): lax.psum((jnp.sum(own_attn * hat_one, axis=0), jnp.sum(own_attn, axis=0),...  43 us
    ppermute x7, starting transfers between devices, turn_regions(): lax.ppermute(blocks_here[tick - 1], axis_name=device_axis, perm=[(pp, (pp...  33.3 us
    reduce_scatter x1, waiting for transfers between devices, local(): lax.psum_scatter(attn_part + mlp_part, 'tp', scatter_dimension=0, tiled=T...  28.9 us
    unnamed x119, local copies, waits for them, and re-layouts  25.8 us
    psum x1, blocking collectives, local(): lax.psum((grad_qkv, qv_bias_grad, grad_dense, grad_up, grad_up_bias, grad...  20.7 us
    ppermute x7, waiting for transfers between devices, turn_regions(): lax.ppermute(blocks_here[tick - 1], axis_name=device_axis, perm=[(pp, (pp...  19 us
  transfers between devices with their start and end apart: 14, of which 11 were waited for; matrix products, arithmetic and copies ran while one was open for 9% of the time, Pallas kernels for 0%

profile of v1, /device:TPU:0, one launch (start us, length us, event | category | flops | bytes accessed | tf_op | source)
XLA Modules:
  0.0 668.6 jit_solution(5007538866163105697)
XLA Ops:
  9.6 1.9 fusion.74
  11.5 10.1 %all_gather.16 = bf16[512,768]{1,0:T(8,128)(2,1)S(1)} all-gather(bf16[128,768]{1,0:T(8,128)(2,1)S(1)} %get-tuple-element.958), channel_id=1, replica_groups=mesh['ctx'=8,'tp'=4] {'tp'}, dimensions={0}, use_global_device_ids=true | all-gather | bytes 983040 | tf_op jit(solution)/shard_map/all_gather | solution.py:78
  25.5 1.6 pad_maximum_fusion.1
  28.1 4.5 collective-permute-start
  32.7 5.8 collective-permute-done
  38.5 5.2 collective-permute-start.1
  43.7 7.4 %all_gather.20 = bf16[512,768]{1,0:T(8,128)(2,1)S(1)} all-gather(bf16[128,768]{1,0:T(8,128)(2,1)} %param.37), channel_id=1, replica_groups=mesh['ctx'=8,'tp'=4] {'tp'}, dimensions={0}, use_global_device_ids=true | all-gather | bytes 983040 | tf_op jit(solution)/shard_map/all_gather | solution.py:185
  51.2 3.5 collective-permute-start.2
  55.2 3.1 collective-permute-done.2
  58.4 4.6 collective-permute-start.3
  64.1 4.6 collective-permute-done.3
  68.7 5.2 collective-permute-start.4
  75.4 1.9 collective-permute-done.4
  77.3 5.1 collective-permute-start.5
  83.9 1.7 collective-permute-done.5
  85.6 5.2 collective-permute-start.6
  92.2 1.7 collective-permute-done.6
  105.0 16.9 %while.39 = (s32[]{:T(128)}, f32[3,512]{1,0:T(4,128)S(1)}, f32[3,512]{1,0:T(4,128)S(1)}, f32[3,512,64]{1,2,0:T(8,128)S(1)}, s32[4]{0:T(128)S(1)}, /*index=5*/s32...) while((s32[]{:T(128)}, f32[3,512]{1,0:T(4,128)S(1)}, ...), condition=%wide.region_8.9_spmd.clone, body=%wide.region_3.8_spmd.clone.sunk | while | flops 424874496 | bytes 22858608 | solution.py:170
  107.6 6.5 conditional.6
  111.1 3.0 fusion.10
  121.9 9.6 %all-gather.5.cloned.1.call-done = bf16[4096,3,64]{0,2,1:T(8,128)(2,1)} async-done(((bf16[512,3,64]{0,2,1:T(8,128)(2,1)}), bf16[4096,3,64]{0,2,1:T(8,128)(2,1)}) %all-gather.5.cloned.1.call-update) | async-done | bytes 1572880 | tf_op jit(solution)/shard_map/all_gather | solution.py:214
  131.5 2.8 copy.75
  136.3 37.3 %while.40 = (s32[]{:T(128)}, f32[512,3,64]{0,2,1:T(8,128)S(1)}, f32[4,1024,384]{2,1,0:T(8,128)}, s32[4]{0:T(128)S(1)}, s32[]{:T(128)}, /*index=5*/s32[]{:T(128)}...) while((s32[]{:T(128)}, f32[512,3,64]{0,2,1:T(8,128)S(1)}, ...), condition=%wide.region_14.15_spmd.clone, body=%wide.region_11.14_spmd.clone.sunk | while | flops 1024722432 | bytes 56325616 | solution.py:263
  138.9 8.3 %conditional.7 = (f32[512,3,64]{0,2,1:T(8,128)S(1)}, f32[1,1024,384]{1,2,0:T(8,128)S(1)}) conditional(s32[]{:T(128)} %convert_element_type.209, f32[512,3,64]{0,2,1:T(8,128)S(1)} %get-tuple-element.1217, (s32[]{:T(128)}, s32[]{:T(128)}, s32[512]{0:T(512)}, bf16[4,1024,3,64]{1,3,2,0:T(8,128)(2,1)S(1)}, s32[]{:T(128)}, ...), branch_computations={%region_12.12_spmd, %region_13.13_spmd} | conditional | flops 1024722432 | bytes 37448308 | solution.py:261
  140.5 3.3 fusion.23
  147.3 1.6 copy.79
  148.9 2.8 constant_dynamic-update-slice_fusion.18
  156.2 2.8 constant_dynamic-update-slice_fusion.18
  163.4 2.8 constant_dynamic-update-slice_fusion.18
  170.7 2.8 constant_dynamic-update-slice_fusion.18
  174.5 8.8 %all_gather.18 = bf16[512,768]{1,0:T(8,128)(2,1)S(1)} all-gather(bf16[128,768]{1,0:T(8,128)(2,1)S(1)} %copy-done.33), channel_id=1, replica_groups=mesh['ctx'=8,'tp'=4] {'tp'}, dimensions={0}, use_global_device_ids=true | all-gather | bytes 983040 | tf_op jit(solution)/shard_map/all_gather | solution.py:79
  183.3 4.2 fusion.44
  189.5 2.0 fusion.93
  193.1 131.7 %reduce-scatter.7.cloned.1.call-done = f32[512,384]{1,0:T(8,128)} async-done(((f32[4096,384]{1,0:T(8,128)}), f32[512,384]{1,0:T(8,128)}) %reduce-scatter.7.cloned.1.call-update) | async-done | bytes 786448 | tf_op jit(solution)/shard_map/reduce_scatter | solution.py:265
  324.7 2.0 slice.122
  326.7 1.8 copy.46
  332.6 2.0 fusion.112
  336.0 1.9 convolution_add_fusion
  339.0 3.3 fusion.91
  342.4 2.2 fusion.114
  346.1 1.8 fusion.59
  349.1 20.7 %all-reduce.1 = (f32[2,192]{1,0:T(2,128)}, f32[768]{0:T(1024)}) all-reduce(f32[2,192]{1,0:T(2,128)S(1)} %pad_maximum_fusion.4, f32[768]{0:T(1024)S(1)} %get-tuple-element.970), channel_id=1, replica_groups=mesh['ctx'=8,'tp'=4] {'ctx'}, use_global_device_ids=true, to_apply=%region_33.34 | all-reduce | flops 1152 | bytes 9216 | tf_op jit(solution)/shard_map/psum | solution.py:300
  369.8 15.1 %reduce-scatter.9.cloned.1.call-done = f32[128,768]{1,0:T(8,128)} async-done(((f32[512,768]{1,0:T(8,128)}), f32[128,768]{1,0:T(8,128)}) %reduce-scatter.9.cloned.1.call-update) | async-done | bytes 393232 | tf_op jit(solution)/shard_map/reduce_scatter | solution.py:285
  386.4 28.9 %reduce-scatter.5.cloned.1.call-done = f32[128,768]{1,0:T(8,128)} async-done(((f32[512,768]{1,0:T(8,128)}), f32[128,768]{1,0:T(8,128)}) %reduce-scatter.5.cloned.1.call-update) | async-done | bytes 393232 | tf_op jit(solution)/shard_map/reduce_scatter | solution.py:181
  415.3 2.3 convert_reduce_fusion.1
  417.6 43.0 %all-reduce = (f32[768]{0:T(1024)}, f32[768]{0:T(1024)}, f32[768]{0:T(1024)}, f32[768]{0:T(1024)}, f32[768]{0:T(1024)S(1)}) all-reduce(f32[768]{0:T(1024)S(1)} %get-tuple-element.862, f32[768]{0:T(1024)S(1)} %get-tuple-element.867, f32[768]{0:T(1024)S(1)} %get-tuple-element.871, ...), channel_id=1, replica_groups=mesh['ctx'=8,'tp'=4] {'ctx','tp'}, use_global_device_ids=true, to_apply=%region_23.24 | all-reduce | flops 3840 | bytes 30720 | tf_op jit(solution)/shard_map/psum | solution.py:290
  460.5 193.0 %all-reduce.5.cloned.1.call-done = (f32[768,3,192]{0,2,1:T(8,128)}, f32[192,768]{1,0:T(8,128)}, f32[768,768]{1,0:T(8,128)}, f32[768,768]{1,0:T(8,128)}) async-done(((f32[768,3,192]{0,2,1:T(8,128)}, f32[192,768]{1,0:T(8,128)}, f32[768,768]{1,0:T(8,128)}, f32[768,768]{1,0:T(8,128)}), (f32[768,3,192]{0,2,1:T(8,128)}, f32[192,768]{1,0:T(8,128)}, f32[768,768]{1,0:T(8,128)}, ...) | async-done | bytes 7077904 | tf_op jit(solution)/shard_map/psum | solution.py:300
  654.1 2.9 copy.135
  (259 shorter events, 66.1 us)
Async XLA Ops:
  7.2 176.1 %copy-start = (bf16[768,768]{1,0:T(8,128)(2,1)S(1)}, bf16[768,768]{1,0:T(8,128)(2,1)}, u32[]{:S(2)}) copy-start(bf16[768,768]{1,0:T(8,128)(2,1)} %param.33) | copy-start | bytes 3538948
  7.2 14.4 %copy-start.12 = (bf16[768,3,192]{0,2,1:T(8,128)(2,1)S(1)}, bf16[768,3,192]{0,2,1:T(8,128)(2,1)}, u32[]{:S(2)}) copy-start(bf16[768,3,192]{0,2,1:T(8,128)(2,1)} %param.29) | copy-start | bytes 2654212
  7.2 96.2 %all-gather.3.cloned.1.call-start = ((), (), s32[]{:S(2)}) async-start(), calls=%async_computation.4 | async-start | bytes 1769472 | tf_op jit(solution)/shard_map/all_gather | solution.py:131
  8.5 13.1 %copy-start.44 = (f32[128]{0:T(128)}, f32[128]{0:T(128)S(1)}, u32[]{:S(2)}) copy-start(f32[128]{0:T(128)S(1)} %broadcast_multiply_fusion.5) | copy-start | bytes 1540
  9.6 12.0 %copy-start.47 = (f32[128]{0:T(128)}, f32[128]{0:T(128)S(1)}, u32[]{:S(2)}) copy-start(f32[128]{0:T(128)S(1)} %add_rsqrt_fusion) | copy-start | bytes 1540
  25.5 37.6 %copy-start.25 = (bf16[192,768]{1,0:T(8,128)(2,1)S(1)}, bf16[192,768]{1,0:T(8,128)(2,1)}, u32[]{:S(2)}) copy-start(bf16[192,768]{1,0:T(8,128)(2,1)} %param.31) | copy-start | bytes 884740
  27.1 104.4 %all-gather.5.cloned.1.call-start = ((), (), s32[]{:S(2)}) async-start(), calls=%async_computation.6 | async-start | bytes 1769472 | tf_op jit(solution)/shard_map/all_gather | solution.py:214
  28.1 4.5 copy-start.19
  28.1 10.4 %collective-permute-start = (bf16[512,3,64]{0,2,1:T(8,128)(2,1)S(1)}, bf16[512,3,64]{0,2,1:T(8,128)(2,1)S(1)}, u32[]{:S(2)}, u32[]{:S(2)}) collective-permute-start(bf16[512,3,64]{0,2,1:T(8,128)(2,1)S(1)} %get-tuple-element.942), channel_id=1, source_target_pairs={{0,28},{4,0},{8,4},{12,8},{16,12},{20,16},{24,20},{28,24},{1,29},{... | collective-permute-start | bytes 589832 | tf_op jit(solution)/shard_map/ppermute | solution.py:139
  32.6 292.1 %reduce-scatter.7.cloned.1.call-start = ((), (), s32[]{:S(2)}) async-start(), calls=%async_computation.7 | async-start | bytes 7077888 | tf_op jit(solution)/shard_map/reduce_scatter | solution.py:265
  38.5 12.6 %collective-permute-start.1 = (bf16[512,3,64]{0,2,1:T(8,128)(2,1)S(1)}, bf16[512,3,64]{0,2,1:T(8,128)(2,1)S(1)}, u32[]{:S(2)}, u32[]{:S(2)}) collective-permute-start(bf16[512,3,64]{0,2,1:T(8,128)(2,1)S(1)} %collective-permute-done), channel_id=1, source_target_pairs={{0,28},{4,0},{8,4},{12,8},{16,12},{20,16},{24,20},{28,24},{1,29},{... | collective-permute-start | bytes 589832 | tf_op jit(solution)/shard_map/ppermute | solution.py:139
  51.1 32.0 %copy-start.3 = (bf16[512,768]{1,0:T(8,128)(2,1)}, bf16[512,768]{1,0:T(8,128)(2,1)S(1)}, u32[]{:S(2)}) copy-start(bf16[512,768]{1,0:T(8,128)(2,1)S(1)} %all_gather.20) | copy-start | bytes 2359300
  51.2 7.2 %collective-permute-start.2 = (bf16[512,3,64]{0,2,1:T(8,128)(2,1)S(1)}, bf16[512,3,64]{0,2,1:T(8,128)(2,1)S(1)}, u32[]{:S(2)}, u32[]{:S(2)}) collective-permute-start(bf16[512,3,64]{0,2,1:T(8,128)(2,1)S(1)} %collective-permute-done.1), channel_id=1, source_target_pairs={{0,28},{4,0},{8,4},{12,8},{16,12},{20,16},{24,20},{28,24},{1,29},{... | collective-permute-start | bytes 589832 | tf_op jit(solution)/shard_map/ppermute | solution.py:139
  58.4 10.4 %collective-permute-start.3 = (bf16[512,3,64]{0,2,1:T(8,128)(2,1)S(1)}, bf16[512,3,64]{0,2,1:T(8,128)(2,1)S(1)}, u32[]{:S(2)}, u32[]{:S(2)}) collective-permute-start(bf16[512,3,64]{0,2,1:T(8,128)(2,1)S(1)} %collective-permute-done.2), channel_id=1, source_target_pairs={{0,28},{4,0},{8,4},{12,8},{16,12},{20,16},{24,20},{28,24},{1,29},{... | collective-permute-start | bytes 589832 | tf_op jit(solution)/shard_map/ppermute | solution.py:139
  64.1 30.6 %copy-start.20 = (bf16[512,3,64]{0,2,1:T(8,128)(2,1)S(1)}, bf16[512,3,64]{0,2,1:T(8,128)(2,1)}, u32[]{:S(2)}) copy-start(bf16[512,3,64]{0,2,1:T(8,128)(2,1)} %copy-done.19) | copy-start | bytes 589828
  68.7 8.6 %collective-permute-start.4 = (bf16[512,3,64]{0,2,1:T(8,128)(2,1)S(1)}, bf16[512,3,64]{0,2,1:T(8,128)(2,1)S(1)}, u32[]{:S(2)}, u32[]{:S(2)}) collective-permute-start(bf16[512,3,64]{0,2,1:T(8,128)(2,1)S(1)} %collective-permute-done.3), channel_id=1, source_target_pairs={{0,28},{4,0},{8,4},{12,8},{16,12},{20,16},{24,20},{28,24},{1,29},{... | collective-permute-start | bytes 589832 | tf_op jit(solution)/shard_map/ppermute | solution.py:139
  77.3 8.3 %collective-permute-start.5 = (bf16[512,3,64]{0,2,1:T(8,128)(2,1)S(1)}, bf16[512,3,64]{0,2,1:T(8,128)(2,1)S(1)}, u32[]{:S(2)}, u32[]{:S(2)}) collective-permute-start(bf16[512,3,64]{0,2,1:T(8,128)(2,1)S(1)} %collective-permute-done.4), channel_id=1, source_target_pairs={{0,28},{4,0},{8,4},{12,8},{16,12},{20,16},{24,20},{28,24},{1,29},{... | collective-permute-start | bytes 589832 | tf_op jit(solution)/shard_map/ppermute | solution.py:139
  85.6 8.4 %collective-permute-start.6 = (bf16[512,3,64]{0,2,1:T(8,128)(2,1)S(1)}, bf16[512,3,64]{0,2,1:T(8,128)(2,1)S(1)}, u32[]{:S(2)}, u32[]{:S(2)}) collective-permute-start(bf16[512,3,64]{0,2,1:T(8,128)(2,1)S(1)} %collective-permute-done.5), channel_id=1, source_target_pairs={{0,28},{4,0},{8,4},{12,8},{16,12},{20,16},{24,20},{28,24},{1,29},{... | collective-permute-start | bytes 589832 | tf_op jit(solution)/shard_map/ppermute | solution.py:139
  121.9 9.6 %copy-start.39 = (s32[512]{0:T(512)}, s32[512]{0:T(512)S(1)}, u32[]{:S(2)}) copy-start(s32[512]{0:T(512)S(1)} %get-tuple-element.1354) | copy-start | bytes 6148
  131.5 3.4 copy-start.30
  136.3 2.6 copy-start.1
  148.9 2.8 copy-start.2
  151.7 2.6 copy-start.1
  156.2 2.8 copy-start.2
  159.0 2.6 copy-start.1
  163.4 2.8 copy-start.2
  166.2 2.6 copy-start.1
  170.7 2.8 copy-start.2
  173.5 9.7 %copy-start.54 = (f32[768]{0:T(1024)S(1)}, f32[768]{0:T(1024)}, u32[]{:S(2)}) copy-start(f32[768]{0:T(1024)} %param.34) | copy-start | bytes 9220
  173.6 196.2 %reduce-scatter.11.cloned.1.call-start = ((), (), s32[]{:S(2)}) async-start(), calls=%async_computation.9 | async-start | bytes 1966080 | tf_op jit(solution)/shard_map/reduce_scatter | solution.py:286
  183.3 4.3 copy-start.7
  183.3 4.3 copy-start.4
  183.3 4.3 copy-start.23
  191.6 193.3 %reduce-scatter.9.cloned.1.call-start = ((), (), s32[]{:S(2)}) async-start(), calls=%async_computation.8 | async-start | bytes 1966080 | tf_op jit(solution)/shard_map/reduce_scatter | solution.py:285
  324.7 3.7 copy-start.18
  334.6 80.6 %reduce-scatter.5.cloned.1.call-start = ((), (), s32[]{:S(2)}) async-start(), calls=%async_computation.5 | async-start | bytes 1966080 | tf_op jit(solution)/shard_map/reduce_scatter | solution.py:181
  337.9 315.6 %all-reduce.5.cloned.1.call-start = ((), (), s32[]{:S(2)}) async-start(), calls=%async_computation.10 | async-start | bytes 14155776 | tf_op jit(solution)/shard_map/psum | solution.py:300
  347.9 36.9 %copy-start.11 = (bf16[128,768]{1,0:T(8,128)(2,1)S(1)}, bf16[128,768]{1,0:T(8,128)(2,1)}, u32[]{:S(2)}) copy-start(bf16[128,768]{1,0:T(8,128)(2,1)} %param.23) | copy-start | bytes 589828
  347.9 36.9 %copy-start.41 = (f32[768]{0:T(1024)S(1)}, f32[768]{0:T(1024)}, u32[]{:S(2)}) copy-start(f32[768]{0:T(1024)} %param.27) | copy-start | bytes 9220
  347.9 36.9 %copy-start.42 = (f32[768]{0:T(1024)S(1)}, f32[768]{0:T(1024)}, u32[]{:S(2)}) copy-start(f32[768]{0:T(1024)} %param.25) | copy-start | bytes 9220
  347.9 36.9 %copy-start.45 = (f32[128]{0:T(128)S(1)}, f32[128]{0:T(128)}, u32[]{:S(2)}) copy-start(f32[128]{0:T(128)} %copy-done.44) | copy-start | bytes 1540
  347.9 36.9 %copy-start.48 = (f32[128]{0:T(128)S(1)}, f32[128]{0:T(128)}, u32[]{:S(2)}) copy-start(f32[128]{0:T(128)} %copy-done.47) | copy-start | bytes 1540
  347.9 67.3 %copy-start.49 = (f32[768]{0:T(1024)S(1)}, f32[768]{0:T(1024)}, u32[]{:S(2)}) copy-start(f32[768]{0:T(1024)} %param.36) | copy-start | bytes 9220
  348.0 67.3 %copy-start.50 = (f32[768]{0:T(1024)S(1)}, f32[768]{0:T(1024)}, u32[]{:S(2)}) copy-start(f32[768]{0:T(1024)} %param.32) | copy-start | bytes 9220
  348.9 66.4 %copy-start.32 = (bf16[128,768]{1,0:T(8,128)(2,1)S(1)}, bf16[128,768]{1,0:T(8,128)(2,1)}, u32[]{:S(2)}) copy-start(bf16[128,768]{1,0:T(8,128)(2,1)} %param.37) | copy-start | bytes 589828
  460.5 196.5 %copy-start.51 = (f32[768]{0:T(1024)}, f32[768]{0:T(1024)S(1)}, u32[]{:S(2)}) copy-start(f32[768]{0:T(1024)S(1)} %get-tuple-element.1287) | copy-start | bytes 9220
  654.1 3.0 copy-start.35
  654.1 3.8 copy-start.17
  (27 other events, 36.6 us)
Sparse Core Ops, SparseCore 0:
  27.2 56.6 all-gather.2
  86.6 44.8 all-gather.4
  173.7 151.0 reduce-scatter.6
  327.1 27.2 reduce-scatter.10
  356.8 27.9 reduce-scatter.8
  387.2 27.9 reduce-scatter.4
  420.8 232.6 all-reduce.4
